TPU v7x, 256 devices: a whole 4x4x8 slice. The times are simulated.
256 devices in a mesh: gx: 16 (over x, z_hi), gy: 8 (over y, core), ga: 2 (over z_lo).
Axes of the slice: x: 4, y: 4, z: 8 (z_hi: 4, z_lo: 2; z = z_hi * 2 + z_lo), core: 2. Of those that a mesh axis runs over, the one named last changes fastest.
Arguments:
- head: float32 [16, 256, 8192], P(None, 'gx', ('gy', 'ga')), may hold values from -6 to 6
- conductivity: float32 [16, 256, 8192], P(None, 'gx', ('gy', 'ga')), may hold values from 0.1 to 10
- root_layer: int32 [256, 8192], P('gx', ('gy', 'ga')), may hold values from 0 to 15
- veg_type: int32 [256, 8192], P('gx', ('gy', 'ga')), may hold values from 0 to 16
- uptake_rate: float32 [17], replicated, may hold values from 0.2 to 2
- depth: float32 [256, 8192], P('gx'), may hold values from 0.05 to 2
- conveyance: float32 [256, 8192], P('gx'), may hold values from 0.2 to 5
- elevation: float32 [256, 8192], P('gx'), may hold values from -3 to 3
- land_mask: int32 [256, 8192], P('gx'), may hold values 0 or 1
Outputs:
- new_head: float32 [16, 256, 8192], P(None, 'gx', ('gy', 'ga'))
- new_depth: float32 [256, 8192], P('gx')
All inputs are finite; a program needn't handle non-finite values. No bound on the sum of `land_mask` on one device may be relied on, other than what follows from the above.
Results may differ from a plain program's by a relative error of at most 0.0003.
Values sent between devices are 32-bit elements; how exact they have to be, the bound alone decides.
A program may use at most 64 MiB of HBM per device.

v0:
```python
import jax
import jax.numpy as jnp
from jax import lax
from jax.sharding import PartitionSpec as P

NVEG = 17
SSW = 4


exchange_coef = 0.5
storage_coef = 0.5


def with_halo(cells, sides, width):
    for axis, dim in sides:
        count = lax.axis_size(axis)
        ends = count - 1
        head = lax.slice_in_dim(cells, 0, width, axis=dim)
        tail = lax.slice_in_dim(cells, cells.shape[dim] - width, cells.shape[dim], axis=dim)
        cells = jnp.concatenate(
            [
                lax.ppermute(tail, axis, [(i, (i + 1) % count) for i in range(ends)]),
                cells,
                lax.ppermute(head, axis, [((i + 1) % count, i) for i in range(ends)]),
            ],
            axis=dim,
        )
    return cells


def harmonic(first, second):
    total = first + second
    return 2.0 * first * second / jnp.where(total > 0, total, 1.0)


def lateral(field_ext, coef_ext):
    center = coef_ext[..., 1:-1, 1:-1]
    wsum = jnp.zeros_like(center)
    nsum = jnp.zeros_like(center)
    for rows, cols in (
        (slice(2, None), slice(1, -1)),
        (slice(None, -2), slice(1, -1)),
        (slice(1, -1), slice(2, None)),
        (slice(1, -1), slice(None, -2)),
    ):
        weight = harmonic(center, coef_ext[..., rows, cols])
        wsum = wsum + weight
        nsum = nsum + weight * field_ext[..., rows, cols]
    return (wsum, nsum)


def guarded(numer, denom):
    return jnp.where(denom > 0, numer / jnp.where(denom > 0, denom, 1.0), 0.0)


def surface_sweep(depth_ext, drag_ext, bed_ext, base, diag):
    wsum, nsum = lateral(depth_ext + bed_ext, drag_ext)
    bed = bed_ext[1:-1, 1:-1]
    return guarded(base + nsum - wsum * bed, diag + wsum)


def soil_sweep(head_ext, cond_ext, base, diag):
    cond = cond_ext[:, 1:-1, 1:-1]
    inner = head_ext[:, 1:-1, 1:-1]
    wsum, nsum = lateral(head_ext, cond_ext)
    vertical = harmonic(cond[:-1], cond[1:])
    blank = jnp.zeros_like(cond[:1])
    down = jnp.concatenate([vertical, blank], axis=0)
    upward = jnp.concatenate([blank, vertical], axis=0)
    below = jnp.concatenate([inner[1:], blank], axis=0)
    above = jnp.concatenate([blank, inner[:-1]], axis=0)
    numer = base + nsum + down * (below - 1.0) + upward * (above + 1.0)
    return guarded(numer, diag + wsum + down + upward)


def widen_cols(stacked, width):
    pads = [(0, 0)] * (stacked.ndim - 1) + [(width, width)]
    return jnp.pad(stacked, pads)


def body(
    head, conductivity, root_layer, veg_type, uptake_rate, depth, conveyance, elevation, land_mask
):
    layers_here, rows_here, cols_here = head.shape
    offset = lax.axis_index(("gy", "ga")) * cols_here
    coupling_rows = exchange_coef * land_mask.astype(jnp.float32)
    coupling = lax.dynamic_slice_in_dim(coupling_rows, offset, cols_here, 1)
    top = head[0]
    top_rows = lax.all_gather(top, ("gy", "ga"), axis=1, tiled=True)
    drag = conveyance * jnp.power(depth, 5.0 / 3.0)
    sbase = depth + coupling_rows * top_rows
    sdiag = 1.0 + coupling_rows
    opened = with_halo(jnp.stack([depth, drag, elevation]), (("gx", 1),), 1)
    opened = widen_cols(opened, 1)
    drag_ext = opened[1]
    bed_ext = opened[2]
    level = surface_sweep(opened[0], drag_ext, bed_ext, sbase, sdiag)
    for sweep in range(SSW - 1):
        level_ext = widen_cols(with_halo(level, (("gx", 0),), 1), 1)
        level = surface_sweep(level_ext, drag_ext, bed_ext, sbase, sdiag)
    level_here = lax.dynamic_slice_in_dim(level, offset, cols_here, 1)
    kinds = jnp.arange(NVEG, dtype=jnp.int32)[:, None, None]
    rate = jnp.sum(jnp.where(veg_type[None] == kinds, uptake_rate[:, None, None], 0.0), axis=0)
    layers = jnp.arange(layers_here, dtype=jnp.int32)[:, None, None]
    inside = (layers <= root_layer[None]).astype(jnp.float32)
    sink = rate[None] * inside / (root_layer[None].astype(jnp.float32) + 1.0)
    base = storage_coef * head - sink
    base = base.at[0].add(coupling * level_here)
    diag = jnp.full(head.shape, storage_coef, jnp.float32)
    diag = diag.at[0].add(coupling)
    opened = with_halo(jnp.stack([head, conductivity]), (("gx", 2), (("gy", "ga"), 3)), 1)
    cond_ext = opened[1]
    current = soil_sweep(opened[0], cond_ext, base, diag)
    head_ext = with_halo(current, (("gx", 1), (("gy", "ga"), 2)), 1)
    current = soil_sweep(head_ext, cond_ext, base, diag)
    return (current, level)


def solution(mesh):
    return jax.shard_map(
        body,
        mesh=mesh,
        in_specs=(
            P(None, "gx", ("gy", "ga")),
            P(None, "gx", ("gy", "ga")),
            P("gx", ("gy", "ga")),
            P("gx", ("gy", "ga")),
            P(),
            P("gx", None),
            P("gx", None),
            P("gx", None),
            P("gx", None),
        ),
        out_specs=(P(None, "gx", ("gy", "ga")), P("gx", None)),
        check_vma=False,
    )
```

profile of v0, /device:TPU:34, one launch (start us, length us, event | category | flops | bytes accessed | tf_op | source)
XLA Modules:
  0.0 151.8 jit_solution(12704075630938351134)
XLA Ops:
  0.7 1.5 %multiply_bitcast_fusion = f32[1,16,8192]{2,1,0:T(8,128)S(1)} fusion(f32[16,8192]{1,0:T(8,128)} %param.19, f32[16,8192]{1,0:T(8,128)} %param.18), kind=kLoop, calls=%fused_computation.125 | loop fusion | flops 131072 | bytes 1572864 | tf_op jit(solution)/shard_map/stack | solution.py:93
  2.2 2.0 %pad_maximum_fusion.18 = (f32[3,1,8192]{2,1,0:T(1,128)}, f32[3,1,8192]{2,1,0:T(1,128)}) fusion(f32[1,16,8192]{2,1,0:T(8,128)} %bitcast.50, f32[1,16,8192]{2,1,0:T(8,128)S(1)} %multiply_bitcast_fusion, f32[1,16,8192]{2,1,0:T(8,128)} %bitcast.42), kind=kLoop, calls=%fused_computation.144 | loop fusion | flops 98304 | bytes 1769472 | tf_op jit(solution)/shard_map/slice | solution.py:19
  4.2 5.2 %collective-permute-start.4 = (f32[3,1,8192]{2,1,0:T(1,128)}, f32[3,1,8192]{2,1,0:T(1,128)}, u32[]{:S(2)}, u32[]{:S(2)}) collective-permute-start(f32[3,1,8192]{2,1,0:T(1,128)} %get-tuple-element.35), channel_id=1, source_target_pairs={{0,16},{16,32},{32,48},{48,64},{64,80},{80,96},{96,112},{112,128},... | collective-permute-start | bytes 294920 | tf_op jit(solution)/shard_map/ppermute | solution.py:22
  9.4 4.0 %collective-permute-start.5 = (f32[3,1,8192]{2,1,0:T(1,128)}, f32[3,1,8192]{2,1,0:T(1,128)}, u32[]{:S(2)}, u32[]{:S(2)}) collective-permute-start(f32[3,1,8192]{2,1,0:T(1,128)} %get-tuple-element.36), channel_id=1, source_target_pairs={{16,0},{32,16},{48,32},{64,48},{80,64},{96,80},{112,96},{128,112},... | collective-permute-start | bytes 294920 | tf_op jit(solution)/shard_map/ppermute | solution.py:24
  13.5 0.1 pad_maximum_fusion.20
  13.6 3.4 %collective-permute-start = (f32[2,16,1,512]{3,2,1,0:T(1,128)S(1)}, f32[2,16,1,512]{3,2,1,0:T(1,128)S(1)}, u32[]{:S(2)}, u32[]{:S(2)}) collective-permute-start(f32[2,16,1,512]{3,2,1,0:T(1,128)S(1)} %get-tuple-element.39), channel_id=1, source_target_pairs={{0,16},{16,32},{32,48},{48,64},{64,80},{80,96},{96,112},{112,128},... | collective-permute-start | bytes 196616 | tf_op jit(solution)/shard_map/ppermute | solution.py:22
  17.0 5.5 %collective-permute-start.1 = (f32[2,16,1,512]{3,2,1,0:T(1,128)S(1)}, f32[2,16,1,512]{3,2,1,0:T(1,128)S(1)}, u32[]{:S(2)}, u32[]{:S(2)}) collective-permute-start(f32[2,16,1,512]{3,2,1,0:T(1,128)S(1)} %get-tuple-element.40), channel_id=1, source_target_pairs={{16,0},{32,16},{48,32},{64,48},{80,64},{96,80},{112,96},{128,112},... | collective-permute-start | bytes 196616 | tf_op jit(solution)/shard_map/ppermute | solution.py:24
  22.5 0.1 select_reduce_fusion
  22.6 0.1 divide_subtract_fusion
  22.7 0.0 collective-permute-done
  22.8 2.6 %collective-permute-done.1 = f32[2,16,1,512]{3,2,1,0:T(1,128)S(1)} collective-permute-done((f32[2,16,1,512]{3,2,1,0:T(1,128)S(1)}, f32[2,16,1,512]{3,2,1,0:T(1,128)S(1)}, u32[]{:S(2)}, u32[]{:S(2)}) %collective-permute-start.1) | collective-permute-done | bytes 65568 | tf_op jit(solution)/shard_map/ppermute | solution.py:24
  25.3 0.2 pad_maximum_fusion.12
  25.6 1.9 %collective-permute-start.2 = (f32[2,16,18,1]{3,2,1,0:T(8,128)S(1)}, f32[2,16,18,1]{3,2,1,0:T(8,128)}, u32[]{:S(2)}, u32[]{:S(2)}) collective-permute-start(f32[2,16,18,1]{3,2,1,0:T(8,128)S(1)} %get-tuple-element.37), channel_id=1, source_target_pairs={{0,1},{1,2},{2,3},{3,4},{4,5},{5,6},{6,7},{7,8},{8,9},{9,10},{10,1... | collective-permute-start | bytes 6920 | tf_op jit(solution)/shard_map/ppermute | solution.py:22
  27.5 4.7 %collective-permute-start.3 = (f32[2,16,18,1]{3,2,1,0:T(8,128)S(1)}, f32[2,16,18,1]{3,2,1,0:T(8,128)}, u32[]{:S(2)}, u32[]{:S(2)}) collective-permute-start(f32[2,16,18,1]{3,2,1,0:T(8,128)S(1)} %get-tuple-element.38), channel_id=1, source_target_pairs={{1,0},{2,1},{3,2},{4,3},{5,4},{6,5},{7,6},{8,7},{9,8},{10,9},{11,1... | collective-permute-start | bytes 6920 | tf_op jit(solution)/shard_map/ppermute | solution.py:24
  32.2 41.6 %all-gather = f32[1,16,8192]{2,1,0:T(8,128)S(1)} all-gather(f32[1,16,512]{2,1,0:T(8,128)S(1)} %slice.287), channel_id=2, replica_groups=mesh['gx'=16,'gy'=8,'ga'=2] {'gy','ga'}, dimensions={2}, use_global_device_ids=true | all-gather | bytes 557056 | tf_op jit(solution)/shard_map/all_gather | solution.py:89
  73.8 0.0 collective-permute-done.2
  73.8 0.0 collective-permute-done.3
  73.8 2.3 %pad_maximum_fusion = f32[2,16,18,514]{3,2,1,0:T(8,128)S(1)} fusion(f32[2,16,18,1]{3,2,1,0:T(8,128)} %collective-permute-done.3, f32[2,16,1,512]{3,2,1,0:T(1,128)S(1)} %collective-permute-done.1, f32[1,16,16,512]{3,2,1,0:T(8,128)S(1)} %bitcast.49, f32[1,16,16,512]{3,2,1,0:T(8,128)S(1)} %bitcast.46, f32[2,16,1,512]{3,2,1,0:T(1,128)S(1)} %collective-permute-done, ...), kind=kLoop, calls=%fused_computation.7 | loop fusion | flops 1480320 | bytes 2368512 | tf_op jit(solution)/shard_map/concatenate | solution.py:20
  76.1 0.0 copy-start
  76.1 0.0 copy-start.4
  76.1 0.1 slice_bitcast_fusion.1
  76.3 0.0 collective-permute-done.4
  76.3 0.0 collective-permute-done.5
  76.3 0.9 copy-done
  77.1 0.2 copy-done.4
  77.3 2.0 %select_maximum_fusion = f32[3,18,8194]{2,1,0:T(8,128)S(1)} fusion(f32[3,1,8192]{2,1,0:T(1,128)} %collective-permute-done.5, f32[3,1,8192]{2,1,0:T(1,128)} %collective-permute-done.4, f32[1,16,8192]{2,1,0:T(8,128)S(1)} %bitcast.51, f32[1,16,8192]{2,1,0:T(8,128)S(1)} %multiply_bitcast_fusion, f32[1,16,8192]{2,1,0:T(8,128)S(1)} %bitcast.43), kind=kLoop, calls=%fused_computation.2 | loop fusion | flops 5309712 | bytes 3539376 | tf_op jit(solution)/shard_map/concatenate | solution.py:20
  79.3 0.0 copy-start.2
  79.4 0.1 slice_bitcast_fusion.4
  79.5 0.1 fusion.4
  79.6 0.8 copy-done.2
  80.4 1.3 fusion.59
  81.8 7.0 %collective-permute-start.6 = (f32[1,8192]{1,0:T(1,128)S(1)}, f32[1,8192]{1,0:T(1,128)S(1)}, u32[]{:S(2)}, u32[]{:S(2)}) collective-permute-start(f32[1,8192]{1,0:T(1,128)S(1)} %get-tuple-element.54), channel_id=1, source_target_pairs={{0,16},{16,32},{32,48},{48,64},{64,80},{80,96},{96,112},{112,128},... | collective-permute-start | bytes 98312 | tf_op jit(solution)/shard_map/ppermute | solution.py:22
  88.7 1.9 %collective-permute-start.7 = (f32[1,8192]{1,0:T(1,128)S(1)}, f32[1,8192]{1,0:T(1,128)S(1)}, u32[]{:S(2)}, u32[]{:S(2)}) collective-permute-start(f32[1,8192]{1,0:T(1,128)S(1)} %get-tuple-element.55), channel_id=1, source_target_pairs={{16,0},{32,16},{48,32},{64,48},{80,64},{96,80},{112,96},{128,112},... | collective-permute-start | bytes 98312 | tf_op jit(solution)/shard_map/ppermute | solution.py:24
  90.7 0.3 fusion.69
  91.0 0.0 collective-permute-done.6
  91.0 4.4 %collective-permute-done.7 = f32[1,8192]{1,0:T(1,128)S(1)} collective-permute-done((f32[1,8192]{1,0:T(1,128)S(1)}, f32[1,8192]{1,0:T(1,128)S(1)}, u32[]{:S(2)}, u32[]{:S(2)}) %collective-permute-start.7) | collective-permute-done | bytes 32800 | tf_op jit(solution)/shard_map/ppermute | solution.py:24
  95.4 0.4 fusion.3
  95.9 0.8 fusion.52
  96.7 3.1 %collective-permute-start.8 = (f32[1,8192]{1,0:T(1,128)S(1)}, f32[1,8192]{1,0:T(1,128)S(1)}, u32[]{:S(2)}, u32[]{:S(2)}) collective-permute-start(f32[1,8192]{1,0:T(1,128)S(1)} %get-tuple-element.52), channel_id=1, source_target_pairs={{0,16},{16,32},{32,48},{48,64},{64,80},{80,96},{96,112},{112,128},... | collective-permute-start | bytes 98312 | tf_op jit(solution)/shard_map/ppermute | solution.py:22
  99.9 5.7 %collective-permute-start.9 = (f32[1,8192]{1,0:T(1,128)S(1)}, f32[1,8192]{1,0:T(1,128)S(1)}, u32[]{:S(2)}, u32[]{:S(2)}) collective-permute-start(f32[1,8192]{1,0:T(1,128)S(1)} %get-tuple-element.53), channel_id=1, source_target_pairs={{16,0},{32,16},{48,32},{64,48},{80,64},{96,80},{112,96},{128,112},... | collective-permute-start | bytes 98312 | tf_op jit(solution)/shard_map/ppermute | solution.py:24
  105.6 0.3 fusion.63
  105.9 0.0 collective-permute-done.8
  105.9 1.2 collective-permute-done.9
  107.2 0.4 fusion.2
  107.6 0.8 fusion.45
  108.4 4.1 %collective-permute-start.10 = (f32[1,8192]{1,0:T(1,128)S(1)}, f32[1,8192]{1,0:T(1,128)S(1)}, u32[]{:S(2)}, u32[]{:S(2)}) collective-permute-start(f32[1,8192]{1,0:T(1,128)S(1)} %get-tuple-element.50), channel_id=1, source_target_pairs={{0,16},{16,32},{32,48},{48,64},{64,80},{80,96},{96,112},{112,128},... | collective-permute-start | bytes 98312 | tf_op jit(solution)/shard_map/ppermute | solution.py:22
  112.5 5.1 %collective-permute-start.11 = (f32[1,8192]{1,0:T(1,128)S(1)}, f32[1,8192]{1,0:T(1,128)S(1)}, u32[]{:S(2)}, u32[]{:S(2)}) collective-permute-start(f32[1,8192]{1,0:T(1,128)S(1)} %get-tuple-element.51), channel_id=1, source_target_pairs={{16,0},{32,16},{48,32},{64,48},{80,64},{96,80},{112,96},{128,112},... | collective-permute-start | bytes 98312 | tf_op jit(solution)/shard_map/ppermute | solution.py:24
  117.6 1.6 %collective-permute-done.11 = f32[1,8192]{1,0:T(1,128)S(1)} collective-permute-done((f32[1,8192]{1,0:T(1,128)S(1)}, f32[1,8192]{1,0:T(1,128)S(1)}, u32[]{:S(2)}, u32[]{:S(2)}) %collective-permute-start.11) | collective-permute-done | bytes 32800 | tf_op jit(solution)/shard_map/ppermute | solution.py:24
  119.2 0.4 fusion.1
  119.6 0.8 fusion.38
  120.4 0.0 copy-start.5
  120.5 1.4 fusion.31
  121.9 0.1 fusion.71
  121.9 7.2 %collective-permute-start.12 = (f32[16,1,512]{2,1,0:T(1,128)S(1)}, f32[16,1,512]{2,1,0:T(1,128)S(1)}, u32[]{:S(2)}, u32[]{:S(2)}) collective-permute-start(f32[16,1,512]{2,1,0:T(1,128)S(1)} %get-tuple-element.48), channel_id=1, source_target_pairs={{16,0},{32,16},{48,32},{64,48},{80,64},{96,80},{112,96},{128,112},... | collective-permute-start | bytes 98312 | tf_op jit(solution)/shard_map/ppermute | solution.py:24
  129.2 1.9 %collective-permute-start.13 = (f32[16,1,512]{2,1,0:T(1,128)S(1)}, f32[16,1,512]{2,1,0:T(1,128)S(1)}, u32[]{:S(2)}, u32[]{:S(2)}) collective-permute-start(f32[16,1,512]{2,1,0:T(1,128)S(1)} %get-tuple-element.47), channel_id=1, source_target_pairs={{0,16},{16,32},{32,48},{48,64},{64,80},{80,96},{96,112},{112,128},... | collective-permute-start | bytes 98312 | tf_op jit(solution)/shard_map/ppermute | solution.py:22
  131.1 0.0 collective-permute-done.12
  131.1 7.0 %collective-permute-done.13 = f32[16,1,512]{2,1,0:T(1,128)S(1)} collective-permute-done((f32[16,1,512]{2,1,0:T(1,128)S(1)}, f32[16,1,512]{2,1,0:T(1,128)S(1)}, u32[]{:S(2)}, u32[]{:S(2)}) %collective-permute-start.13) | collective-permute-done | bytes 32800 | tf_op jit(solution)/shard_map/ppermute | solution.py:22
  138.1 0.2 pad_maximum_fusion.15
  138.3 1.9 %collective-permute-start.14 = (f32[16,18,1]{2,1,0:T(8,128)S(1)}, f32[16,18,1]{2,1,0:T(8,128)S(1)}, u32[]{:S(2)}, u32[]{:S(2)}) collective-permute-start(f32[16,18,1]{2,1,0:T(8,128)S(1)} %get-tuple-element.43), channel_id=1, source_target_pairs={{1,0},{2,1},{3,2},{4,3},{5,4},{6,5},{7,6},{8,7},{9,8},{10,9},{11,1... | collective-permute-start | bytes 3464 | tf_op jit(solution)/shard_map/ppermute | solution.py:24
  140.2 3.6 %collective-permute-start.15 = (f32[16,18,1]{2,1,0:T(8,128)S(1)}, f32[16,18,1]{2,1,0:T(8,128)S(1)}, u32[]{:S(2)}, u32[]{:S(2)}) collective-permute-start(f32[16,18,1]{2,1,0:T(8,128)S(1)} %get-tuple-element.44), channel_id=1, source_target_pairs={{0,1},{1,2},{2,3},{3,4},{4,5},{5,6},{6,7},{7,8},{8,9},{9,10},{10,1... | collective-permute-start | bytes 3464 | tf_op jit(solution)/shard_map/ppermute | solution.py:22
  143.8 0.1 fusion.70
  144.0 1.3 collective-permute-done.14
  145.3 4.2 %collective-permute-done.15 = f32[16,18,1]{2,1,0:T(8,128)S(1)} collective-permute-done((f32[16,18,1]{2,1,0:T(8,128)S(1)}, f32[16,18,1]{2,1,0:T(8,128)S(1)}, u32[]{:S(2)}, u32[]{:S(2)}) %collective-permute-start.15) | collective-permute-done | bytes 1184 | tf_op jit(solution)/shard_map/ppermute | solution.py:22
  149.5 2.3 %fusion.20 = f32[16,16,512]{2,1,0:T(8,128)} fusion(f32[16,16,512]{2,1,0:T(8,128)S(1)} %fusion.64, f32[16,18,1]{2,1,0:T(8,128)S(1)} %collective-permute-done.15, f32[16,1,512]{2,1,0:T(1,128)S(1)} %collective-permute-done.12, f32[16,16,512]{2,1,0:T(8,128)S(1)} %fusion.31, f32[16,1,512]{2,1,0:T(1,128)S(1)} %collective-permute-done.13, ...), kind=kLoop, calls=%fused_computation.52 | loop fusion | flops 6946816 | bytes 5769472 | tf_op jit(solution)/shard_map/jit(_where)/select_n | solution.py:53
  (19 shorter events, 0.2 us)
Async XLA Ops:
  0.6 12.8 %copy-start.1 = (f32[16,16,512]{2,1,0:T(8,128)S(1)}, f32[16,16,512]{2,1,0:T(8,128)}, u32[]{:S(2)}) copy-start(f32[16,16,512]{2,1,0:T(8,128)} %param.13) | copy-start | bytes 1572868
  0.6 12.8 %copy-start.3 = (f32[16,16,512]{2,1,0:T(8,128)S(1)}, f32[16,16,512]{2,1,0:T(8,128)}, u32[]{:S(2)}) copy-start(f32[16,16,512]{2,1,0:T(8,128)} %param.14) | copy-start | bytes 1572868
  0.7 21.8 %copy-start.6 = (s32[16,512]{1,0:T(8,128)S(1)}, s32[16,512]{1,0:T(8,128)}, u32[]{:S(2)}) copy-start(s32[16,512]{1,0:T(8,128)} %param.15) | copy-start | bytes 98308
  0.7 21.8 %copy-start.7 = (s32[16,512]{1,0:T(8,128)S(1)}, s32[16,512]{1,0:T(8,128)}, u32[]{:S(2)}) copy-start(s32[16,512]{1,0:T(8,128)} %param.16) | copy-start | bytes 98308
  0.7 21.8 %copy-start.8 = (f32[17]{0:T(128)S(1)}, f32[17]{0:T(128)}, u32[]{:S(2)}) copy-start(f32[17]{0:T(128)} %param.17) | copy-start | bytes 208
  4.2 72.0 %collective-permute-start.4 = (f32[3,1,8192]{2,1,0:T(1,128)}, f32[3,1,8192]{2,1,0:T(1,128)}, u32[]{:S(2)}, u32[]{:S(2)}) collective-permute-start(f32[3,1,8192]{2,1,0:T(1,128)} %get-tuple-element.35), channel_id=1, source_target_pairs={{0,16},{16,32},{32,48},{48,64},{64,80},{80,96},{96,112},{112,128},... | collective-permute-start | bytes 294920 | tf_op jit(solution)/shard_map/ppermute | solution.py:22
  9.4 66.9 %collective-permute-start.5 = (f32[3,1,8192]{2,1,0:T(1,128)}, f32[3,1,8192]{2,1,0:T(1,128)}, u32[]{:S(2)}, u32[]{:S(2)}) collective-permute-start(f32[3,1,8192]{2,1,0:T(1,128)} %get-tuple-element.36), channel_id=1, source_target_pairs={{16,0},{32,16},{48,32},{64,48},{80,64},{96,80},{112,96},{128,112},... | collective-permute-start | bytes 294920 | tf_op jit(solution)/shard_map/ppermute | solution.py:24
  13.6 9.2 %collective-permute-start = (f32[2,16,1,512]{3,2,1,0:T(1,128)S(1)}, f32[2,16,1,512]{3,2,1,0:T(1,128)S(1)}, u32[]{:S(2)}, u32[]{:S(2)}) collective-permute-start(f32[2,16,1,512]{3,2,1,0:T(1,128)S(1)} %get-tuple-element.39), channel_id=1, source_target_pairs={{0,16},{16,32},{32,48},{48,64},{64,80},{80,96},{96,112},{112,128},... | collective-permute-start | bytes 196616 | tf_op jit(solution)/shard_map/ppermute | solution.py:22
  17.0 8.4 %collective-permute-start.1 = (f32[2,16,1,512]{3,2,1,0:T(1,128)S(1)}, f32[2,16,1,512]{3,2,1,0:T(1,128)S(1)}, u32[]{:S(2)}, u32[]{:S(2)}) collective-permute-start(f32[2,16,1,512]{3,2,1,0:T(1,128)S(1)} %get-tuple-element.40), channel_id=1, source_target_pairs={{16,0},{32,16},{48,32},{64,48},{80,64},{96,80},{112,96},{128,112},... | collective-permute-start | bytes 196616 | tf_op jit(solution)/shard_map/ppermute | solution.py:24
  25.6 48.2 %collective-permute-start.2 = (f32[2,16,18,1]{3,2,1,0:T(8,128)S(1)}, f32[2,16,18,1]{3,2,1,0:T(8,128)}, u32[]{:S(2)}, u32[]{:S(2)}) collective-permute-start(f32[2,16,18,1]{3,2,1,0:T(8,128)S(1)} %get-tuple-element.37), channel_id=1, source_target_pairs={{0,1},{1,2},{2,3},{3,4},{4,5},{5,6},{6,7},{7,8},{8,9},{9,10},{10,1... | collective-permute-start | bytes 6920 | tf_op jit(solution)/shard_map/ppermute | solution.py:22
  27.5 46.3 %collective-permute-start.3 = (f32[2,16,18,1]{3,2,1,0:T(8,128)S(1)}, f32[2,16,18,1]{3,2,1,0:T(8,128)}, u32[]{:S(2)}, u32[]{:S(2)}) collective-permute-start(f32[2,16,18,1]{3,2,1,0:T(8,128)S(1)} %get-tuple-element.38), channel_id=1, source_target_pairs={{1,0},{2,1},{3,2},{4,3},{5,4},{6,5},{7,6},{8,7},{9,8},{10,9},{11,1... | collective-permute-start | bytes 6920 | tf_op jit(solution)/shard_map/ppermute | solution.py:24
  76.1 1.0 copy-start
  76.1 1.2 copy-start.4
  79.3 1.0 copy-start.2
  81.8 9.2 %collective-permute-start.6 = (f32[1,8192]{1,0:T(1,128)S(1)}, f32[1,8192]{1,0:T(1,128)S(1)}, u32[]{:S(2)}, u32[]{:S(2)}) collective-permute-start(f32[1,8192]{1,0:T(1,128)S(1)} %get-tuple-element.54), channel_id=1, source_target_pairs={{0,16},{16,32},{32,48},{48,64},{64,80},{80,96},{96,112},{112,128},... | collective-permute-start | bytes 98312 | tf_op jit(solution)/shard_map/ppermute | solution.py:22
  88.7 6.7 %collective-permute-start.7 = (f32[1,8192]{1,0:T(1,128)S(1)}, f32[1,8192]{1,0:T(1,128)S(1)}, u32[]{:S(2)}, u32[]{:S(2)}) collective-permute-start(f32[1,8192]{1,0:T(1,128)S(1)} %get-tuple-element.55), channel_id=1, source_target_pairs={{16,0},{32,16},{48,32},{64,48},{80,64},{96,80},{112,96},{128,112},... | collective-permute-start | bytes 98312 | tf_op jit(solution)/shard_map/ppermute | solution.py:24
  96.7 9.2 %collective-permute-start.8 = (f32[1,8192]{1,0:T(1,128)S(1)}, f32[1,8192]{1,0:T(1,128)S(1)}, u32[]{:S(2)}, u32[]{:S(2)}) collective-permute-start(f32[1,8192]{1,0:T(1,128)S(1)} %get-tuple-element.52), channel_id=1, source_target_pairs={{0,16},{16,32},{32,48},{48,64},{64,80},{80,96},{96,112},{112,128},... | collective-permute-start | bytes 98312 | tf_op jit(solution)/shard_map/ppermute | solution.py:22
  99.9 7.3 %collective-permute-start.9 = (f32[1,8192]{1,0:T(1,128)S(1)}, f32[1,8192]{1,0:T(1,128)S(1)}, u32[]{:S(2)}, u32[]{:S(2)}) collective-permute-start(f32[1,8192]{1,0:T(1,128)S(1)} %get-tuple-element.53), channel_id=1, source_target_pairs={{16,0},{32,16},{48,32},{64,48},{80,64},{96,80},{112,96},{128,112},... | collective-permute-start | bytes 98312 | tf_op jit(solution)/shard_map/ppermute | solution.py:24
  108.4 9.2 %collective-permute-start.10 = (f32[1,8192]{1,0:T(1,128)S(1)}, f32[1,8192]{1,0:T(1,128)S(1)}, u32[]{:S(2)}, u32[]{:S(2)}) collective-permute-start(f32[1,8192]{1,0:T(1,128)S(1)} %get-tuple-element.50), channel_id=1, source_target_pairs={{0,16},{16,32},{32,48},{48,64},{64,80},{80,96},{96,112},{112,128},... | collective-permute-start | bytes 98312 | tf_op jit(solution)/shard_map/ppermute | solution.py:22
  112.5 6.7 %collective-permute-start.11 = (f32[1,8192]{1,0:T(1,128)S(1)}, f32[1,8192]{1,0:T(1,128)S(1)}, u32[]{:S(2)}, u32[]{:S(2)}) collective-permute-start(f32[1,8192]{1,0:T(1,128)S(1)} %get-tuple-element.51), channel_id=1, source_target_pairs={{16,0},{32,16},{48,32},{64,48},{80,64},{96,80},{112,96},{128,112},... | collective-permute-start | bytes 98312 | tf_op jit(solution)/shard_map/ppermute | solution.py:24
  120.4 1.5 copy-start.5
  121.9 9.2 %collective-permute-start.12 = (f32[16,1,512]{2,1,0:T(1,128)S(1)}, f32[16,1,512]{2,1,0:T(1,128)S(1)}, u32[]{:S(2)}, u32[]{:S(2)}) collective-permute-start(f32[16,1,512]{2,1,0:T(1,128)S(1)} %get-tuple-element.48), channel_id=1, source_target_pairs={{16,0},{32,16},{48,32},{64,48},{80,64},{96,80},{112,96},{128,112},... | collective-permute-start | bytes 98312 | tf_op jit(solution)/shard_map/ppermute | solution.py:24
  129.2 8.9 %collective-permute-start.13 = (f32[16,1,512]{2,1,0:T(1,128)S(1)}, f32[16,1,512]{2,1,0:T(1,128)S(1)}, u32[]{:S(2)}, u32[]{:S(2)}) collective-permute-start(f32[16,1,512]{2,1,0:T(1,128)S(1)} %get-tuple-element.47), channel_id=1, source_target_pairs={{0,16},{16,32},{32,48},{48,64},{64,80},{80,96},{96,112},{112,128},... | collective-permute-start | bytes 98312 | tf_op jit(solution)/shard_map/ppermute | solution.py:22
  138.3 7.0 %collective-permute-start.14 = (f32[16,18,1]{2,1,0:T(8,128)S(1)}, f32[16,18,1]{2,1,0:T(8,128)S(1)}, u32[]{:S(2)}, u32[]{:S(2)}) collective-permute-start(f32[16,18,1]{2,1,0:T(8,128)S(1)} %get-tuple-element.43), channel_id=1, source_target_pairs={{1,0},{2,1},{3,2},{4,3},{5,4},{6,5},{7,6},{8,7},{9,8},{10,9},{11,1... | collective-permute-start | bytes 3464 | tf_op jit(solution)/shard_map/ppermute | solution.py:24
  140.2 9.3 %collective-permute-start.15 = (f32[16,18,1]{2,1,0:T(8,128)S(1)}, f32[16,18,1]{2,1,0:T(8,128)S(1)}, u32[]{:S(2)}, u32[]{:S(2)}) collective-permute-start(f32[16,18,1]{2,1,0:T(8,128)S(1)} %get-tuple-element.44), channel_id=1, source_target_pairs={{0,1},{1,2},{2,3},{3,4},{4,5},{5,6},{6,7},{7,8},{8,9},{9,10},{10,1... | collective-permute-start | bytes 3464 | tf_op jit(solution)/shard_map/ppermute | solution.py:22
where the time goes:
time: 152 us
  starting transfers between devices  66.2 us (44%)
  blocking collectives  41.6 us (27%)
  waiting for transfers between devices  22.3 us (15%)
  other arithmetic  17.7 us (12%)
  local copies, waits for them, and re-layouts  2.78 us (2%)
    all_gather x1, blocking collectives, body(): top_rows = lax.all_gather(top, ('gy', 'ga'), axis=1, tiled=True)  41.6 us
    ppermute x8, starting transfers between devices, with_halo(): lax.ppermute(head, axis, [((i + 1) % count, i) for i in range(ends)])  36 us
    ppermute x8, starting transfers between devices, with_halo(): lax.ppermute(tail, axis, [(i, (i + 1) % count) for i in range(ends)])  30.2 us
    ppermute x8, waiting for transfers between devices, with_halo(): lax.ppermute(tail, axis, [(i, (i + 1) % count) for i in range(ends)])  11.2 us
    ppermute x8, waiting for transfers between devices, with_halo(): lax.ppermute(head, axis, [((i + 1) % count, i) for i in range(ends)])  11.1 us
    select_n x6, other arithmetic, guarded(): return jnp.where(denom > 0, numer / jnp.where(denom > 0, denom, 1.0), 0.0)  7.39 us
    concatenate x2, other arithmetic, with_halo(): jnp.concatenate([lax.ppermute(tail, axis, [(i, (i + 1) % count) for i in...  4.3 us
  transfers between devices with their start and end apart: 16, of which 7 were waited for; matrix products, arithmetic and copies ran while one was open for 2% of the time, Pallas kernels for 0%

commit v1 on v0

v1 whole, which is shorter than its diff:
```python
import functools

import jax
import jax.numpy as jnp
from jax import lax
from jax.experimental import pallas as pl
from jax.experimental.pallas import tpu as pltpu
from jax.sharding import PartitionSpec as P

NVEG = 17
SSW = 4
RING = 4
LANES = 128
EDGE = 2 * LANES

exchange_coef = 0.5
storage_coef = 0.5
MESH = pl.DeviceIdType.MESH


def harmonic(first, second):
    total = first + second
    return 2.0 * first * second / jnp.where(total > 0, total, 1.0)


def lane_of(shape):
    return lax.broadcasted_iota(jnp.int32, shape, len(shape) - 1)


def row_of(shape):
    return lax.broadcasted_iota(jnp.int32, shape, len(shape) - 2)


def from_right(x, edge):
    width = x.shape[1]
    y = pltpu.roll(x, width - 1, 1)
    tail = jnp.where(lane_of(edge.shape) == LANES - 1, edge, y[:, width - LANES :])
    return jnp.concatenate([y[:, : width - LANES], tail], axis=1)


def from_left(x, edge):
    y = pltpu.roll(x, 1, 1)
    front = jnp.where(lane_of(edge.shape) == 0, edge, y[:, :LANES])
    return jnp.concatenate([front, y[:, LANES:]], axis=1)


def circular(window, cols):
    left = window[:, :LANES]
    right = window[:, cols + LANES :]
    side = jnp.where(lane_of(left.shape) < LANES // 2, right, left)
    return jnp.concatenate([window[:, LANES : cols + LANES], side], axis=1)


def kernel(
    head, cond, root, veg, uptake, depth, conv, elev, mask,
    new_head, new_depth,
    hx, cx, px, qx, root_v, veg_v, field, mask_v, top_v, level_v, cpl_v, sink_v,
    wr_v, wl_v, wu_v, wv_v, inv_v, base_v,
    pack_s, pack_r, pack2_s, pack2_r,
    load_sem, send_sem, recv_sem, gsend_sem, grecv_sem, out_sem,
):
    layers, rows, cols = head.shape
    gx = lax.axis_index("gx")
    gy = lax.axis_index("gy")
    ga = lax.axis_index("ga")
    ngx = lax.axis_size("gx")
    nga = lax.axis_size("ga")
    ncol = lax.axis_size("gy") * nga
    col = gy * nga + ga
    off = pl.multiple_of(col * cols, LANES)
    total = ncol * cols

    def at(dx, dc):
        c = lax.rem(col + dc + ncol, ncol)
        return (lax.rem(gx + dx + ngx, ngx), c // nga, lax.rem(c, nga))

    left_off = pl.multiple_of(lax.rem(off - LANES + total, total), LANES)
    right_off = pl.multiple_of(lax.rem(off + cols, total), LANES)
    loads = []
    for n, src in enumerate((depth, conv, elev)):
        loads.append(pltpu.make_async_copy(src.at[:, pl.ds(left_off, LANES)], field.at[n, 0:rows, 0:LANES], load_sem.at[3 * n]))
        loads.append(pltpu.make_async_copy(src.at[:, pl.ds(off, cols)], field.at[n, 0:rows, LANES : LANES + cols], load_sem.at[3 * n + 1]))
        loads.append(pltpu.make_async_copy(src.at[:, pl.ds(right_off, LANES)], field.at[n, 0:rows, LANES + cols :], load_sem.at[3 * n + 2]))
    loads.append(pltpu.make_async_copy(mask.at[:, pl.ds(left_off, LANES)], mask_v.at[0:rows, 0:LANES], load_sem.at[9]))
    loads.append(pltpu.make_async_copy(mask.at[:, pl.ds(off, cols)], mask_v.at[0:rows, LANES : LANES + cols], load_sem.at[10]))
    loads.append(pltpu.make_async_copy(mask.at[:, pl.ds(right_off, LANES)], mask_v.at[0:rows, LANES + cols :], load_sem.at[11]))
    loads.append(pltpu.make_async_copy(head.at[0], top_v.at[0:rows, LANES : LANES + cols], load_sem.at[12]))
    loads.append(pltpu.make_async_copy(root, root_v, load_sem.at[13]))
    loads.append(pltpu.make_async_copy(veg, veg_v, load_sem.at[14]))
    for c in loads:
        c.start()
    for r in range(rows):
        pltpu.make_async_copy(head.at[:, r, :], hx.at[r + 1], load_sem.at[15]).start()
        pltpu.make_async_copy(cond.at[:, r, :], cx.at[r + 1], load_sem.at[16]).start()

    barrier = pltpu.get_barrier_semaphore()
    peers = [at(0, d) for d in range(1, ncol)]
    peers += [at(1, 0), at(-1, 0), at(1, 1), at(1, -1), at(-1, 1), at(-1, -1)]
    for peer in peers:
        pl.semaphore_signal(barrier, inc=1, device_id=peer, device_id_type=MESH)
    for c in loads:
        c.wait()
    pl.semaphore_wait(barrier, len(peers))

    sent = []
    count = [0]

    def send(src, dst, device):
        n = count[0]
        count[0] += 1
        c = pltpu.make_async_remote_copy(
            src_ref=src, dst_ref=dst, send_sem=send_sem.at[n], recv_sem=recv_sem.at[n],
            device_id=device, device_id_type=MESH,
        )
        c.start()
        sent.append(c)
        return c

    lo = pl.ds(rows, RING)
    hi = pl.ds(rows + RING, RING)
    first = pl.ds(0, RING)
    last = pl.ds(rows - RING, RING)
    own = pl.ds(LANES, cols)
    lt = pl.ds(0, LANES)
    rt = pl.ds(LANES + cols, LANES)
    hl = pl.ds(0, LANES)
    hr = pl.ds(cols - LANES, LANES)
    surface = [
        send(field.at[:, last, :], field.at[:, hi, :], at(1, 0)),
        send(field.at[:, first, :], field.at[:, lo, :], at(-1, 0)),
        send(mask_v.at[last, :], mask_v.at[hi, :], at(1, 0)),
        send(mask_v.at[first, :], mask_v.at[lo, :], at(-1, 0)),
        send(head.at[0, last, :], top_v.at[hi, own], at(1, 0)),
        send(head.at[0, first, :], top_v.at[lo, own], at(-1, 0)),
        send(head.at[0, last, hr], top_v.at[hi, lt], at(1, 1)),
        send(head.at[0, last, hl], top_v.at[hi, rt], at(1, -1)),
        send(head.at[0, first, hr], top_v.at[lo, lt], at(-1, 1)),
        send(head.at[0, first, hl], top_v.at[lo, rt], at(-1, -1)),
        send(head.at[0, :, hr], top_v.at[pl.ds(0, rows), lt], at(0, 1)),
        send(head.at[0, :, hl], top_v.at[pl.ds(0, rows), rt], at(0, -1)),
    ]

    pltpu.make_async_copy(hx.at[pl.ds(1, rows)], hx.at[pl.ds(1, rows)], load_sem.at[15]).wait()
    pltpu.make_async_copy(cx.at[pl.ds(1, rows)], cx.at[pl.ds(1, rows)], load_sem.at[16]).wait()
    soil = [
        send(hx.at[rows], hx.at[0], at(1, 0)),
        send(cx.at[rows], cx.at[0], at(1, 0)),
        send(hx.at[1], hx.at[rows + 1], at(-1, 0)),
        send(cx.at[1], cx.at[rows + 1], at(-1, 0)),
    ]

    def pack(fields, out):
        to_right = jnp.zeros((layers, LANES), jnp.float32)
        to_left = jnp.zeros((layers, LANES), jnp.float32)
        lane = lane_of((layers, LANES))
        for n, ref in enumerate(fields):
            for r in range(rows):
                slot = n * rows + r
                tail = pltpu.roll(ref[r + 1, :, cols - LANES : cols], (slot + 1) % LANES, 1)
                to_right = jnp.where(lane == slot, tail, to_right)
                front = ref[r + 1, :, 0:LANES]
                front = pltpu.roll(front, slot, 1) if slot else front
                to_left = jnp.where(lane == slot, front, to_left)
        out[0] = to_right
        out[1] = to_left

    pack((hx, cx), pack_s)
    soil += [
        send(pack_s.at[0], pack_r.at[0], at(0, 1)),
        send(pack_s.at[1], pack_r.at[1], at(0, -1)),
    ]

    rate = jnp.zeros((rows, cols), jnp.float32)
    kinds = veg_v[...]
    for k in range(NVEG):
        rate = jnp.where(kinds == k, uptake[k], rate)
    sink_v[...] = rate / (root_v[...].astype(jnp.float32) + 1.0)

    for c in surface:
        c.wait_recv()
    high = rows + 2 * RING
    wide = cols + LANES
    rowi = row_of((high, wide))
    lane = lane_of((high, wide))
    outside = (rowi >= rows) & (rowi < rows + RING) & (gx == ngx - 1)
    outside |= (rowi >= rows + RING) & (gx == 0)
    outside |= (lane >= cols) & (lane < cols + LANES // 2) & (col == ncol - 1)
    outside |= (lane >= cols + LANES // 2) & (col == 0)
    dep = circular(field[0], cols)
    con = circular(field[1], cols)
    bed = circular(field[2], cols)
    cpl = exchange_coef * circular(mask_v[...], cols).astype(jnp.float32)
    top = circular(top_v[...], cols)
    drag = con * jnp.exp(jnp.log(dep) * (5.0 / 3.0))
    drag = jnp.where(outside, 0.0, drag)
    w_r = harmonic(drag, pltpu.roll(drag, wide - 1, 1))
    w_l = pltpu.roll(w_r, 1, 1)
    w_d = harmonic(drag, pltpu.roll(drag, high - 1, 0))
    w_u = pltpu.roll(w_d, 1, 0)
    wsum = (w_r + w_l) + (w_d + w_u)
    inv = 1.0 / (1.0 + cpl + wsum)
    part = (dep + cpl * top - wsum * bed) * inv
    w_r = w_r * inv
    w_l = w_l * inv
    w_d = w_d * inv
    w_u = w_u * inv
    level = dep
    for _ in range(SSW):
        t = level + bed
        level = part + (
            (w_r * pltpu.roll(t, wide - 1, 1) + w_l * pltpu.roll(t, 1, 1))
            + (w_d * pltpu.roll(t, high - 1, 0) + w_u * pltpu.roll(t, 1, 0))
        )
    block = level[0:rows, 0:cols]
    level_v[...] = block
    coupling = cpl[0:rows, 0:cols]
    cpl_v[0] = coupling
    cpl_v[1] = coupling * block

    gather = []
    for d in range(1, ncol):
        c = pltpu.make_async_remote_copy(
            src_ref=level_v, dst_ref=new_depth.at[:, pl.ds(off, cols)],
            send_sem=gsend_sem.at[d - 1], recv_sem=grecv_sem.at[d - 1],
            device_id=at(0, d), device_id_type=MESH,
        )
        c.start()
        gather.append(c)
    mine = pltpu.make_async_copy(level_v, new_depth.at[:, pl.ds(off, cols)], out_sem.at[0])
    mine.start()

    for c in soil:
        c.wait_recv()
    has_up = jnp.where(gx > 0, 1.0, 0.0)
    has_down = jnp.where(gx < ngx - 1, 1.0, 0.0)
    has_left = jnp.where(col > 0, 1.0, 0.0)
    has_right = jnp.where(col < ncol - 1, 1.0, 0.0)
    layer = row_of((layers, cols))
    lane0 = lane_of((layers, LANES)) == 0

    def right_edge(packed, slot):
        return pltpu.roll(packed, lax.rem(2 * LANES - 1 - slot, LANES), 1)

    def left_edge(packed, slot):
        return pltpu.roll(packed, lax.rem(2 * LANES - slot, LANES), 1)

    def first_sweep(r, w_up):
        c0 = cx[r + 1]
        h0 = hx[r + 1]
        w_down = harmonic(c0, cx[r + 2]) * jnp.where(r == rows - 1, has_down, 1.0)
        edge_r = right_edge(pack_r[1], rows + r) * has_right
        edge_l = left_edge(pack_r[0], rows + r) * has_left
        w_right = harmonic(c0, from_right(c0, edge_r))
        w_left = from_left(w_right, harmonic(c0[:, :LANES], edge_l))
        w_below = jnp.where(layer == layers - 1, 0.0, harmonic(c0, pltpu.roll(c0, layers - 1, 0)))
        w_above = pltpu.roll(w_below, 1, 0)
        on_top = layer == 0
        coupled = jnp.where(on_top, cpl_v[0, pl.ds(r, 1), :], 0.0)
        source = jnp.where(on_top, cpl_v[1, pl.ds(r, 1), :], 0.0)
        uptake_here = jnp.where(layer <= root_v[pl.ds(r, 1), :], sink_v[pl.ds(r, 1), :], 0.0)
        inv_here = 1.0 / (
            (storage_coef + coupled) + ((w_right + w_left) + (w_up + w_down)) + (w_below + w_above)
        )
        base = (storage_coef * h0 - uptake_here + source) + (w_above - w_below)
        wr_v[r] = w_right
        wl_v[r] = w_left
        wu_v[r] = w_up
        wv_v[r] = w_below
        inv_v[r] = inv_here
        base_v[r] = base
        acc = base + w_right * from_right(h0, right_edge(pack_r[1], r)) + w_left * from_left(h0, left_edge(pack_r[0], r))
        acc += w_up * hx[r] + w_down * hx[r + 2]
        acc += w_below * pltpu.roll(h0, layers - 1, 0) + w_above * pltpu.roll(h0, 1, 0)
        px[r + 1] = acc * inv_here
        return w_down

    wu_v[rows] = lax.fori_loop(0, rows, first_sweep, harmonic(cx[0], cx[1]) * has_up)

    second = [
        send(px.at[rows], px.at[0], at(1, 0)),
        send(px.at[1], px.at[rows + 1], at(-1, 0)),
    ]
    pack((px,), pack2_s)
    second += [
        send(pack2_s.at[0], pack2_r.at[0], at(0, 1)),
        send(pack2_s.at[1], pack2_r.at[1], at(0, -1)),
    ]
    for c in second:
        c.wait_recv()

    def second_sweep(r, carry):
        p0 = px[r + 1]
        w_below = wv_v[r]
        w_above = pltpu.roll(w_below, 1, 0)
        acc = base_v[r] + wr_v[r] * from_right(p0, right_edge(pack2_r[1], r)) + wl_v[r] * from_left(p0, left_edge(pack2_r[0], r))
        acc += wu_v[r] * px[r] + wu_v[r + 1] * px[r + 2]
        acc += w_below * pltpu.roll(p0, layers - 1, 0) + w_above * pltpu.roll(p0, 1, 0)
        qx[r] = acc * inv_v[r]
        return carry

    lax.fori_loop(0, rows, second_sweep, 0)
    for r in range(rows):
        pltpu.make_async_copy(qx.at[r], new_head.at[:, r, :], out_sem.at[1]).start()

    for c in sent:
        c.wait_send()
    for c in gather:
        c.wait()
    mine.wait()
    pltpu.make_async_copy(qx, qx, out_sem.at[1]).wait()


def body(head, conductivity, root_layer, veg_type, uptake_rate, depth, conveyance, elevation, land_mask):
    layers, rows, cols = head.shape
    ncol = lax.axis_size("gy") * lax.axis_size("ga")
    f32 = jnp.float32
    slab = (rows, layers, cols)
    ext = (rows + 2, layers, cols)
    hbm = pl.BlockSpec(memory_space=pl.ANY)
    window = (rows + 2 * RING, cols + EDGE)
    return pl.pallas_call(
        kernel,
        out_shape=(
            jax.ShapeDtypeStruct(head.shape, f32),
            jax.ShapeDtypeStruct(depth.shape, f32),
        ),
        in_specs=[hbm] * 4 + [pl.BlockSpec(memory_space=pltpu.SMEM)] + [hbm] * 4,
        out_specs=(hbm, hbm),
        scratch_shapes=[
            pltpu.VMEM(ext, f32),
            pltpu.VMEM(ext, f32),
            pltpu.VMEM(ext, f32),
            pltpu.VMEM(slab, f32),
            pltpu.VMEM((rows, cols), jnp.int32),
            pltpu.VMEM((rows, cols), jnp.int32),
            pltpu.VMEM((3,) + window, f32),
            pltpu.VMEM(window, jnp.int32),
            pltpu.VMEM(window, f32),
            pltpu.VMEM((rows, cols), f32),
            pltpu.VMEM((2, rows, cols), f32),
            pltpu.VMEM((rows, cols), f32),
            pltpu.VMEM(slab, f32),
            pltpu.VMEM(slab, f32),
            pltpu.VMEM((rows + 1, layers, cols), f32),
            pltpu.VMEM(slab, f32),
            pltpu.VMEM(slab, f32),
            pltpu.VMEM(slab, f32),
            pltpu.VMEM((2, layers, LANES), f32),
            pltpu.VMEM((2, layers, LANES), f32),
            pltpu.VMEM((2, layers, LANES), f32),
            pltpu.VMEM((2, layers, LANES), f32),
            pltpu.SemaphoreType.DMA((17,)),
            pltpu.SemaphoreType.DMA((22,)),
            pltpu.SemaphoreType.DMA((22,)),
            pltpu.SemaphoreType.DMA((ncol - 1,)),
            pltpu.SemaphoreType.DMA((ncol - 1,)),
            pltpu.SemaphoreType.DMA((2,)),
        ],
        compiler_params=pltpu.CompilerParams(collective_id=0, has_side_effects=True),
        name="watershed_step",
    )(head, conductivity, root_layer, veg_type, uptake_rate, depth, conveyance, elevation, land_mask)


def solution(mesh):
    return jax.shard_map(
        body,
        mesh=mesh,
        in_specs=(
            P(None, "gx", ("gy", "ga")),
            P(None, "gx", ("gy", "ga")),
            P("gx", ("gy", "ga")),
            P("gx", ("gy", "ga")),
            P(),
            P("gx", None),
            P("gx", None),
            P("gx", None),
            P("gx", None),
        ),
        out_specs=(P(None, "gx", ("gy", "ga")), P("gx", None)),
        check_vma=False,
    )
```

time: 152 us -> 37 us (0.24)
  the two profiles are of different devices: /device:TPU:34 before, /device:TPU:1 now
where the time goes in v1:
time: 37 us; the launch traced here: 36.8 us
  Pallas kernels  33.4 us (90%)
  local copies, waits for them, and re-layouts  2.74 us (7%)
  between operations  0.65 us (2%)
    pallas_call x1, Pallas kernels, body(): pl.pallas_call(kernel, out_shape=(jax.ShapeDtypeStruct(head.shape, f32),...  33.4 us
    unnamed x4, local copies, waits for them, and re-layouts  2.74 us

profile of v1, /device:TPU:1, one launch (start us, length us, event | category | flops | bytes accessed | tf_op | source)
XLA Modules:
  0.0 36.8 jit_solution(15940690842231115771)
XLA Ops:
  0.6 33.4 %watershed_step.1 = (f32[16,16,512]{2,1,0:T(8,128)}, f32[16,8192]{1,0:T(8,128)}) custom-call(f32[16,16,512]{2,1,0:T(8,128)} %head.1, f32[16,16,512]{2,1,0:T(8,128)} %cond.1, s32[16,512]{1,0:T(8,128)} %root.1, s32[16,512]{1,0:T(8,128)} %veg.1, f32[17]{0:T(128)} %uptake.1, f32[16,8192]{1,0:T(8,128)} %depth.1, f32[16,8192]{1,0:T(8,128)} %conv.1, ...), custom_call_target="tpu_custom_call" | custom-call | tf_op jit(solution)/shard_map/watershed_step/pallas_call | solution.py:321
  34.0 0.0 copy-start
  34.0 1.9 %copy.13 = f32[16,16,512]{2,1,0:T(8,128)} copy(f32[16,16,512]{2,1,0:T(8,128)} %get-tuple-element.4) | data formatting | bytes 1048576
  36.0 0.0 copy-done
  36.0 0.8 %copy.14 = f32[16,8192]{1,0:T(8,128)} copy(f32[16,8192]{1,0:T(8,128)S(1)} %copy-done) | data formatting | bytes 1048576
Async XLA Ops:
  34.0 2.0 %copy-start = (f32[16,8192]{1,0:T(8,128)S(1)}, f32[16,8192]{1,0:T(8,128)}, u32[]{:S(2)}) copy-start(f32[16,8192]{1,0:T(8,128)} %get-tuple-element.5) | copy-start | bytes 1572868

commit v2 on v1

--- a/solution.py
+++ b/solution.py
@@ -54,10 +54,10 @@
 def kernel(
     head, cond, root, veg, uptake, depth, conv, elev, mask,
     new_head, new_depth,
-    hx, cx, px, qx, root_v, veg_v, field, mask_v, top_v, level_v, cpl_v, sink_v,
+    hx, cx, px, qx, root_v, veg_v, field, mask_v, top_v, cpl_v, sink_v,
     wr_v, wl_v, wu_v, wv_v, inv_v, base_v,
     pack_s, pack_r, pack2_s, pack2_r,
-    load_sem, send_sem, recv_sem, gsend_sem, grecv_sem, out_sem,
+    load_sem, send_sem, recv_sem, gsend_sem, grecv_sem, rsend_sem, rrecv_sem, out_sem,
 ):
     layers, rows, cols = head.shape
     gx = lax.axis_index("gx")
@@ -73,6 +73,25 @@
     def at(dx, dc):
         c = lax.rem(col + dc + ncol, ncol)
         return (lax.rem(gx + dx + ngx, ngx), c // nga, lax.rem(c, nga))
+
+    ngy = lax.axis_size("gy")
+
+    def same_core(dy, dz):
+        return (gx, lax.rem(gy + 2 * dy + ngy, ngy), lax.rem(ga + dz + nga, nga))
+
+    def block_cols(device):
+        return pl.ds(pl.multiple_of((device[1] * nga + device[2]) * cols, LANES), cols)
+
+    chips = sorted(
+        ((dy, dz) for dy in range(ngy // 2) for dz in range(nga) if (dy, dz) != (0, 0)),
+        key=lambda v: min(v[0], ngy // 2 - v[0]) + v[1],
+    )
+    partner = (gx, gy + 1 - 2 * lax.rem(gy, 2), ga)
+    barrier = pltpu.get_barrier_semaphore()
+    peers = [at(1, 0), at(-1, 0), at(1, 1), at(1, -1), at(-1, 1), at(-1, -1), at(0, 1), at(0, -1), partner]
+    peers += [same_core(*v) for v in chips]
+    for peer in peers:
+        pl.semaphore_signal(barrier, inc=1, device_id=peer, device_id_type=MESH)
 
     left_off = pl.multiple_of(lax.rem(off - LANES + total, total), LANES)
     right_off = pl.multiple_of(lax.rem(off + cols, total), LANES)
@@ -92,12 +111,6 @@
     for r in range(rows):
         pltpu.make_async_copy(head.at[:, r, :], hx.at[r + 1], load_sem.at[15]).start()
         pltpu.make_async_copy(cond.at[:, r, :], cx.at[r + 1], load_sem.at[16]).start()
-
-    barrier = pltpu.get_barrier_semaphore()
-    peers = [at(0, d) for d in range(1, ncol)]
-    peers += [at(1, 0), at(-1, 0), at(1, 1), at(1, -1), at(-1, 1), at(-1, -1)]
-    for peer in peers:
-        pl.semaphore_signal(barrier, inc=1, device_id=peer, device_id_type=MESH)
     for c in loads:
         c.wait()
     pl.semaphore_wait(barrier, len(peers))
@@ -139,15 +152,71 @@
         send(head.at[0, :, hr], top_v.at[pl.ds(0, rows), lt], at(0, 1)),
         send(head.at[0, :, hl], top_v.at[pl.ds(0, rows), rt], at(0, -1)),
     ]
+    soil = [
+        send(head.at[:, rows - 1, :], hx.at[0], at(1, 0)),
+        send(cond.at[:, rows - 1, :], cx.at[0], at(1, 0)),
+        send(head.at[:, 0, :], hx.at[rows + 1], at(-1, 0)),
+        send(cond.at[:, 0, :], cx.at[rows + 1], at(-1, 0)),
+    ]
+
+    def surface_block(high, outside):
+        wide = cols + LANES
+        dep = circular(field[0, 0:high, :], cols)
+        con = circular(field[1, 0:high, :], cols)
+        bed = circular(field[2, 0:high, :], cols)
+        cpl = exchange_coef * circular(mask_v[0:high, :], cols).astype(jnp.float32)
+        top = circular(top_v[0:high, :], cols)
+        drag = con * jnp.exp(jnp.log(dep) * (5.0 / 3.0))
+        lane = lane_of((high, wide))
+        outside |= (lane >= cols) & (lane < cols + LANES // 2) & (col == ncol - 1)
+        outside |= (lane >= cols + LANES // 2) & (col == 0)
+        drag = jnp.where(outside, 0.0, drag)
+        w_r = harmonic(drag, pltpu.roll(drag, wide - 1, 1))
+        w_l = pltpu.roll(w_r, 1, 1)
+        w_d = harmonic(drag, pltpu.roll(drag, high - 1, 0))
+        w_u = pltpu.roll(w_d, 1, 0)
+        wsum = (w_r + w_l) + (w_d + w_u)
+        inv = 1.0 / (1.0 + cpl + wsum)
+        part = (dep + cpl * top - wsum * bed) * inv
+        w_r = w_r * inv
+        w_l = w_l * inv
+        w_d = w_d * inv
+        w_u = w_u * inv
+        level = dep
+        for _ in range(SSW):
+            t = level + bed
+            level = part + (
+                (w_r * pltpu.roll(t, wide - 1, 1) + w_l * pltpu.roll(t, 1, 1))
+                + (w_d * pltpu.roll(t, high - 1, 0) + w_u * pltpu.roll(t, 1, 0))
+            )
+        return level, cpl
+
+    def spread():
+        mine = block_cols((gx, gy, ga))
+        out = []
+        for n, device in enumerate([partner] + [same_core(*v) for v in chips]):
+            c = pltpu.make_async_remote_copy(
+                src_ref=new_depth.at[:, mine], dst_ref=new_depth.at[:, mine],
+                send_sem=gsend_sem.at[n], recv_sem=grecv_sem.at[n],
+                device_id=device, device_id_type=MESH,
+            )
+            c.start()
+            out.append(c)
+        return out
+
+    def relay(n):
+        dy, dz = chips[n]
+        theirs = block_cols(same_core(-dy, -dz))
+        c = pltpu.make_async_remote_copy(
+            src_ref=new_depth.at[:, theirs], dst_ref=new_depth.at[:, theirs],
+            send_sem=rsend_sem.at[n], recv_sem=rrecv_sem.at[n],
+            device_id=partner, device_id_type=MESH,
+        )
+        c.start()
+        return c
 
     pltpu.make_async_copy(hx.at[pl.ds(1, rows)], hx.at[pl.ds(1, rows)], load_sem.at[15]).wait()
     pltpu.make_async_copy(cx.at[pl.ds(1, rows)], cx.at[pl.ds(1, rows)], load_sem.at[16]).wait()
-    soil = [
-        send(hx.at[rows], hx.at[0], at(1, 0)),
-        send(cx.at[rows], cx.at[0], at(1, 0)),
-        send(hx.at[1], hx.at[rows + 1], at(-1, 0)),
-        send(cx.at[1], cx.at[rows + 1], at(-1, 0)),
-    ]
 
     def pack(fields, out):
         to_right = jnp.zeros((layers, LANES), jnp.float32)
@@ -179,55 +248,16 @@
     for c in surface:
         c.wait_recv()
     high = rows + 2 * RING
-    wide = cols + LANES
-    rowi = row_of((high, wide))
-    lane = lane_of((high, wide))
+    rowi = row_of((high, cols + LANES))
     outside = (rowi >= rows) & (rowi < rows + RING) & (gx == ngx - 1)
     outside |= (rowi >= rows + RING) & (gx == 0)
-    outside |= (lane >= cols) & (lane < cols + LANES // 2) & (col == ncol - 1)
-    outside |= (lane >= cols + LANES // 2) & (col == 0)
-    dep = circular(field[0], cols)
-    con = circular(field[1], cols)
-    bed = circular(field[2], cols)
-    cpl = exchange_coef * circular(mask_v[...], cols).astype(jnp.float32)
-    top = circular(top_v[...], cols)
-    drag = con * jnp.exp(jnp.log(dep) * (5.0 / 3.0))
-    drag = jnp.where(outside, 0.0, drag)
-    w_r = harmonic(drag, pltpu.roll(drag, wide - 1, 1))
-    w_l = pltpu.roll(w_r, 1, 1)
-    w_d = harmonic(drag, pltpu.roll(drag, high - 1, 0))
-    w_u = pltpu.roll(w_d, 1, 0)
-    wsum = (w_r + w_l) + (w_d + w_u)
-    inv = 1.0 / (1.0 + cpl + wsum)
-    part = (dep + cpl * top - wsum * bed) * inv
-    w_r = w_r * inv
-    w_l = w_l * inv
-    w_d = w_d * inv
-    w_u = w_u * inv
-    level = dep
-    for _ in range(SSW):
-        t = level + bed
-        level = part + (
-            (w_r * pltpu.roll(t, wide - 1, 1) + w_l * pltpu.roll(t, 1, 1))
-            + (w_d * pltpu.roll(t, high - 1, 0) + w_u * pltpu.roll(t, 1, 0))
-        )
+    level, cpl = surface_block(high, outside)
     block = level[0:rows, 0:cols]
-    level_v[...] = block
+    new_depth[:, block_cols((gx, gy, ga))] = block
+    gather = spread()
     coupling = cpl[0:rows, 0:cols]
     cpl_v[0] = coupling
     cpl_v[1] = coupling * block
-
-    gather = []
-    for d in range(1, ncol):
-        c = pltpu.make_async_remote_copy(
-            src_ref=level_v, dst_ref=new_depth.at[:, pl.ds(off, cols)],
-            send_sem=gsend_sem.at[d - 1], recv_sem=grecv_sem.at[d - 1],
-            device_id=at(0, d), device_id_type=MESH,
-        )
-        c.start()
-        gather.append(c)
-    mine = pltpu.make_async_copy(level_v, new_depth.at[:, pl.ds(off, cols)], out_sem.at[0])
-    mine.start()
 
     for c in soil:
         c.wait_recv()
@@ -285,6 +315,10 @@
         send(pack2_s.at[0], pack2_r.at[0], at(0, 1)),
         send(pack2_s.at[1], pack2_r.at[1], at(0, -1)),
     ]
+    relays = []
+    for n in range(len(chips)):
+        gather[n + 1].wait_recv()
+        relays.append(relay(n))
     for c in second:
         c.wait_recv()
 
@@ -296,23 +330,24 @@
         acc += wu_v[r] * px[r] + wu_v[r + 1] * px[r + 2]
         acc += w_below * pltpu.roll(p0, layers - 1, 0) + w_above * pltpu.roll(p0, 1, 0)
         qx[r] = acc * inv_v[r]
+        pltpu.make_async_copy(qx.at[r], new_head.at[:, r, :], out_sem.at[0]).start()
         return carry
 
     lax.fori_loop(0, rows, second_sweep, 0)
-    for r in range(rows):
-        pltpu.make_async_copy(qx.at[r], new_head.at[:, r, :], out_sem.at[1]).start()
-
     for c in sent:
         c.wait_send()
     for c in gather:
+        c.wait_send()
+    gather[0].wait_recv()
+    for c in relays:
         c.wait()
-    mine.wait()
-    pltpu.make_async_copy(qx, qx, out_sem.at[1]).wait()
+    pltpu.make_async_copy(qx, qx, out_sem.at[0]).wait()
 
 
 def body(head, conductivity, root_layer, veg_type, uptake_rate, depth, conveyance, elevation, land_mask):
     layers, rows, cols = head.shape
     ncol = lax.axis_size("gy") * lax.axis_size("ga")
+    near = ncol // 2 - 1
     f32 = jnp.float32
     slab = (rows, layers, cols)
     ext = (rows + 2, layers, cols)
@@ -320,12 +355,9 @@
     window = (rows + 2 * RING, cols + EDGE)
     return pl.pallas_call(
         kernel,
-        out_shape=(
-            jax.ShapeDtypeStruct(head.shape, f32),
-            jax.ShapeDtypeStruct(depth.shape, f32),
-        ),
+        out_shape=(pltpu.VMEM(head.shape, f32), pltpu.VMEM(depth.shape, f32)),
         in_specs=[hbm] * 4 + [pl.BlockSpec(memory_space=pltpu.SMEM)] + [hbm] * 4,
-        out_specs=(hbm, hbm),
+        out_specs=(pl.BlockSpec(memory_space=pltpu.VMEM),) * 2,
         scratch_shapes=[
             pltpu.VMEM(ext, f32),
             pltpu.VMEM(ext, f32),
@@ -336,7 +368,6 @@
             pltpu.VMEM((3,) + window, f32),
             pltpu.VMEM(window, jnp.int32),
             pltpu.VMEM(window, f32),
-            pltpu.VMEM((rows, cols), f32),
             pltpu.VMEM((2, rows, cols), f32),
             pltpu.VMEM((rows, cols), f32),
             pltpu.VMEM(slab, f32),
@@ -352,9 +383,11 @@
             pltpu.SemaphoreType.DMA((17,)),
             pltpu.SemaphoreType.DMA((22,)),
             pltpu.SemaphoreType.DMA((22,)),
-            pltpu.SemaphoreType.DMA((ncol - 1,)),
-            pltpu.SemaphoreType.DMA((ncol - 1,)),
-            pltpu.SemaphoreType.DMA((2,)),
+            pltpu.SemaphoreType.DMA((near + 1,)),
+            pltpu.SemaphoreType.DMA((near + 1,)),
+            pltpu.SemaphoreType.DMA((near,)),
+            pltpu.SemaphoreType.DMA((near,)),
+            pltpu.SemaphoreType.DMA((1,)),
         ],
         compiler_params=pltpu.CompilerParams(collective_id=0, has_side_effects=True),
         name="watershed_step",

time: 37 us -> 32.1 us (0.87)
  Pallas kernels: 33.4 us -> 29.3 us
  local copies, waits for them, and re-layouts: 2.74 us -> 1.59 us
    pallas_call x1, Pallas kernels: 33.4 us -> 29.3 us  [body(): pl.pallas_call(kernel, out_shape=(pltpu.VMEM(head.shape, f32), pltpu.VMEM...]
    unnamed x4 -> x2, local copies, waits for them, and re-layouts: 2.74 us -> 1.59 us
where the time goes in v2:
time: 32.1 us; the launch traced here: 31.5 us
  Pallas kernels  29.3 us (91%)
  local copies, waits for them, and re-layouts  1.59 us (5%)
  between operations  0.64 us (2%)
    pallas_call x1, Pallas kernels, body(): pl.pallas_call(kernel, out_shape=(pltpu.VMEM(head.shape, f32), pltpu.VMEM...  29.3 us
    unnamed x2, local copies, waits for them, and re-layouts  1.59 us

profile of v2, /device:TPU:1, one launch (start us, length us, event | category | flops | bytes accessed | tf_op | source)
XLA Modules:
  0.0 31.5 jit_solution(10148632241812263987)
XLA Ops:
  0.6 29.3 %watershed_step.1 = (f32[16,16,512]{2,1,0:T(8,128)S(1)}, f32[16,8192]{1,0:T(8,128)S(1)}) custom-call(f32[16,16,512]{2,1,0:T(8,128)} %head.1, f32[16,16,512]{2,1,0:T(8,128)} %cond.1, s32[16,512]{1,0:T(8,128)} %root.1, s32[16,512]{1,0:T(8,128)} %veg.1, f32[17]{0:T(128)} %uptake.1, f32[16,8192]{1,0:T(8,128)} %depth.1, f32[16,8192]{1,0:T(8,128)} %conv.1, ...), custom_call_target="tpu_custom_call" | custom-call | tf_op jit(solution)/shard_map/watershed_step/pallas_call | solution.py:356
  29.9 0.8 %copy.13 = f32[16,16,512]{2,1,0:T(8,128)} copy(f32[16,16,512]{2,1,0:T(8,128)S(1)} %get-tuple-element.2) | data formatting | bytes 1048576
  30.7 0.8 %copy.14 = f32[16,8192]{1,0:T(8,128)} copy(f32[16,8192]{1,0:T(8,128)S(1)} %get-tuple-element.3) | data formatting | bytes 1048576

commit v3 on v2

--- a/solution.py
+++ b/solution.py
@@ -88,10 +88,29 @@
     )
     partner = (gx, gy + 1 - 2 * lax.rem(gy, 2), ga)
     barrier = pltpu.get_barrier_semaphore()
-    peers = [at(1, 0), at(-1, 0), at(1, 1), at(1, -1), at(-1, 1), at(-1, -1), at(0, 1), at(0, -1), partner]
-    peers += [same_core(*v) for v in chips]
-    for peer in peers:
-        pl.semaphore_signal(barrier, inc=1, device_id=peer, device_id_type=MESH)
+    up, down = gx > 0, gx < ngx - 1
+    left, right = col > 0, col < ncol - 1
+    ways = {
+        (1, 0): (at(1, 0), down, up),
+        (-1, 0): (at(-1, 0), up, down),
+        (0, 1): (at(0, 1), right, left),
+        (0, -1): (at(0, -1), left, right),
+        (1, 1): (at(1, 1), down & right, up & left),
+        (1, -1): (at(1, -1), down & left, up & right),
+        (-1, 1): (at(-1, 1), up & right, down & left),
+        (-1, -1): (at(-1, -1), up & left, down & right),
+    }
+
+    def greet(device):
+        pl.semaphore_signal(barrier, inc=1, device_id=device, device_id_type=MESH)
+
+    for device, there, _ in ways.values():
+        pl.when(there)(functools.partial(greet, device))
+    always = [partner] + [same_core(*v) for v in chips]
+    for device in always:
+        greet(device)
+    present = [there.astype(jnp.int32) for _, there, _ in ways.values()]
+    n_peers = functools.reduce(lambda p, q: p + q, present) + len(always)
 
     left_off = pl.multiple_of(lax.rem(off - LANES + total, total), LANES)
     right_off = pl.multiple_of(lax.rem(off + cols, total), LANES)
@@ -111,23 +130,76 @@
     for r in range(rows):
         pltpu.make_async_copy(head.at[:, r, :], hx.at[r + 1], load_sem.at[15]).start()
         pltpu.make_async_copy(cond.at[:, r, :], cx.at[r + 1], load_sem.at[16]).start()
+
+    def blank(*refs):
+        for ref in refs:
+            ref[...] = jnp.zeros(ref.shape, ref.dtype)
+
+    low_rows = pl.ds(rows, RING)
+    high_rows = pl.ds(rows + RING, RING)
+    tall = rows + 2 * RING
+
+    @pl.when(gx == 0)
+    def _():
+        blank(hx.at[0], cx.at[0], px.at[0], top_v.at[high_rows], mask_v.at[high_rows])
+        field[:, rows + RING : tall, :] = jnp.zeros((3, RING, cols + EDGE), jnp.float32)
+
+    @pl.when(gx == ngx - 1)
+    def _():
+        blank(hx.at[rows + 1], cx.at[rows + 1], px.at[rows + 1], top_v.at[low_rows], mask_v.at[low_rows])
+        field[:, rows : rows + RING, :] = jnp.zeros((3, RING, cols + EDGE), jnp.float32)
+
+    @pl.when(col == 0)
+    def _():
+        blank(pack_r.at[0], pack2_r.at[0], top_v.at[:, pl.ds(0, LANES)])
+
+    @pl.when(col == ncol - 1)
+    def _():
+        blank(pack_r.at[1], pack2_r.at[1], top_v.at[:, pl.ds(LANES + cols, LANES)])
+
     for c in loads:
         c.wait()
-    pl.semaphore_wait(barrier, len(peers))
+    pl.semaphore_wait(barrier, n_peers)
 
     sent = []
     count = [0]
 
-    def send(src, dst, device):
-        n = count[0]
-        count[0] += 1
-        c = pltpu.make_async_remote_copy(
-            src_ref=src, dst_ref=dst, send_sem=send_sem.at[n], recv_sem=recv_sem.at[n],
-            device_id=device, device_id_type=MESH,
-        )
-        c.start()
-        sent.append(c)
-        return c
+    def send(way, *pairs):
+        device, there, from_there = ways[way]
+        copies = []
+        for src, dst in pairs:
+            n = count[0]
+            count[0] += 1
+            copies.append(
+                pltpu.make_async_remote_copy(
+                    src_ref=src, dst_ref=dst, send_sem=send_sem.at[n], recv_sem=recv_sem.at[n],
+                    device_id=device, device_id_type=MESH,
+                )
+            )
+
+        @pl.when(there)
+        def _():
+            for c in copies:
+                c.start()
+
+        sent.append((there, from_there, copies))
+        return sent[-1]
+
+    def arrived(groups):
+        for _, from_there, copies in groups:
+
+            @pl.when(from_there)
+            def _():
+                for c in copies:
+                    c.wait_recv()
+
+    def gone(groups):
+        for there, _, copies in groups:
+
+            @pl.when(there)
+            def _():
+                for c in copies:
+                    c.wait_send()
 
     lo = pl.ds(rows, RING)
     hi = pl.ds(rows + RING, RING)
@@ -138,25 +210,38 @@
     rt = pl.ds(LANES + cols, LANES)
     hl = pl.ds(0, LANES)
     hr = pl.ds(cols - LANES, LANES)
+    every = pl.ds(0, rows)
     surface = [
-        send(field.at[:, last, :], field.at[:, hi, :], at(1, 0)),
-        send(field.at[:, first, :], field.at[:, lo, :], at(-1, 0)),
-        send(mask_v.at[last, :], mask_v.at[hi, :], at(1, 0)),
-        send(mask_v.at[first, :], mask_v.at[lo, :], at(-1, 0)),
-        send(head.at[0, last, :], top_v.at[hi, own], at(1, 0)),
-        send(head.at[0, first, :], top_v.at[lo, own], at(-1, 0)),
-        send(head.at[0, last, hr], top_v.at[hi, lt], at(1, 1)),
-        send(head.at[0, last, hl], top_v.at[hi, rt], at(1, -1)),
-        send(head.at[0, first, hr], top_v.at[lo, lt], at(-1, 1)),
-        send(head.at[0, first, hl], top_v.at[lo, rt], at(-1, -1)),
-        send(head.at[0, :, hr], top_v.at[pl.ds(0, rows), lt], at(0, 1)),
-        send(head.at[0, :, hl], top_v.at[pl.ds(0, rows), rt], at(0, -1)),
+        send(
+            (1, 0),
+            (field.at[:, last, :], field.at[:, hi, :]),
+            (mask_v.at[last, :], mask_v.at[hi, :]),
+            (head.at[0, last, :], top_v.at[hi, own]),
+        ),
+        send(
+            (-1, 0),
+            (field.at[:, first, :], field.at[:, lo, :]),
+            (mask_v.at[first, :], mask_v.at[lo, :]),
+            (head.at[0, first, :], top_v.at[lo, own]),
+        ),
+        send((1, 1), (head.at[0, last, hr], top_v.at[hi, lt])),
+        send((1, -1), (head.at[0, last, hl], top_v.at[hi, rt])),
+        send((-1, 1), (head.at[0, first, hr], top_v.at[lo, lt])),
+        send((-1, -1), (head.at[0, first, hl], top_v.at[lo, rt])),
+        send((0, 1), (head.at[0, :, hr], top_v.at[every, lt])),
+        send((0, -1), (head.at[0, :, hl], top_v.at[every, rt])),
     ]
     soil = [
-        send(head.at[:, rows - 1, :], hx.at[0], at(1, 0)),
-        send(cond.at[:, rows - 1, :], cx.at[0], at(1, 0)),
-        send(head.at[:, 0, :], hx.at[rows + 1], at(-1, 0)),
-        send(cond.at[:, 0, :], cx.at[rows + 1], at(-1, 0)),
+        send(
+            (1, 0),
+            (head.at[:, rows - 1, :], hx.at[0]),
+            (cond.at[:, rows - 1, :], cx.at[0]),
+        ),
+        send(
+            (-1, 0),
+            (head.at[:, 0, :], hx.at[rows + 1]),
+            (cond.at[:, 0, :], cx.at[rows + 1]),
+        ),
     ]
 
     def surface_block(high, outside):
@@ -235,8 +320,8 @@
 
     pack((hx, cx), pack_s)
     soil += [
-        send(pack_s.at[0], pack_r.at[0], at(0, 1)),
-        send(pack_s.at[1], pack_r.at[1], at(0, -1)),
+        send((0, 1), (pack_s.at[0], pack_r.at[0])),
+        send((0, -1), (pack_s.at[1], pack_r.at[1])),
     ]
 
     rate = jnp.zeros((rows, cols), jnp.float32)
@@ -245,8 +330,7 @@
         rate = jnp.where(kinds == k, uptake[k], rate)
     sink_v[...] = rate / (root_v[...].astype(jnp.float32) + 1.0)
 
-    for c in surface:
-        c.wait_recv()
+    arrived(surface)
     high = rows + 2 * RING
     rowi = row_of((high, cols + LANES))
     outside = (rowi >= rows) & (rowi < rows + RING) & (gx == ngx - 1)
@@ -259,8 +343,7 @@
     cpl_v[0] = coupling
     cpl_v[1] = coupling * block
 
-    for c in soil:
-        c.wait_recv()
+    arrived(soil)
     has_up = jnp.where(gx > 0, 1.0, 0.0)
     has_down = jnp.where(gx < ngx - 1, 1.0, 0.0)
     has_left = jnp.where(col > 0, 1.0, 0.0)
@@ -307,20 +390,19 @@
     wu_v[rows] = lax.fori_loop(0, rows, first_sweep, harmonic(cx[0], cx[1]) * has_up)
 
     second = [
-        send(px.at[rows], px.at[0], at(1, 0)),
-        send(px.at[1], px.at[rows + 1], at(-1, 0)),
+        send((1, 0), (px.at[rows], px.at[0])),
+        send((-1, 0), (px.at[1], px.at[rows + 1])),
     ]
     pack((px,), pack2_s)
     second += [
-        send(pack2_s.at[0], pack2_r.at[0], at(0, 1)),
-        send(pack2_s.at[1], pack2_r.at[1], at(0, -1)),
+        send((0, 1), (pack2_s.at[0], pack2_r.at[0])),
+        send((0, -1), (pack2_s.at[1], pack2_r.at[1])),
     ]
     relays = []
     for n in range(len(chips)):
         gather[n + 1].wait_recv()
         relays.append(relay(n))
-    for c in second:
-        c.wait_recv()
+    arrived(second)
 
     def second_sweep(r, carry):
         p0 = px[r + 1]
@@ -334,8 +416,7 @@
         return carry
 
     lax.fori_loop(0, rows, second_sweep, 0)
-    for c in sent:
-        c.wait_send()
+    gone(sent)
     for c in gather:
         c.wait_send()
     gather[0].wait_recv()

time: 32.1 us -> 29.9 us (0.931)
  the two profiles are of different devices: /device:TPU:1 before, /device:TPU:23 now
where the time goes in v3:
time: 29.9 us; the launch traced here: 29.7 us
  Pallas kernels  27.4 us (92%)
  local copies, waits for them, and re-layouts  1.59 us (5%)
  between operations  0.64 us (2%)
    pallas_call x1, Pallas kernels, body(): pl.pallas_call(kernel, out_shape=(pltpu.VMEM(head.shape, f32), pltpu.VMEM...  27.4 us
    unnamed x2, local copies, waits for them, and re-layouts  1.59 us

profile of v3, /device:TPU:23, one launch (start us, length us, event | category | flops | bytes accessed | tf_op | source)
XLA Modules:
  0.0 29.7 jit_solution(5408812142374812066)
XLA Ops:
  0.6 27.4 %watershed_step.1 = (f32[16,16,512]{2,1,0:T(8,128)S(1)}, f32[16,8192]{1,0:T(8,128)S(1)}) custom-call(f32[16,16,512]{2,1,0:T(8,128)} %head.1, f32[16,16,512]{2,1,0:T(8,128)} %cond.1, s32[16,512]{1,0:T(8,128)} %root.1, s32[16,512]{1,0:T(8,128)} %veg.1, f32[17]{0:T(128)} %uptake.1, f32[16,8192]{1,0:T(8,128)} %depth.1, f32[16,8192]{1,0:T(8,128)} %conv.1, ...), custom_call_target="tpu_custom_call" | custom-call | tf_op jit(solution)/shard_map/watershed_step/pallas_call | solution.py:437
  28.1 0.8 %copy.13 = f32[16,16,512]{2,1,0:T(8,128)} copy(f32[16,16,512]{2,1,0:T(8,128)S(1)} %get-tuple-element.2) | data formatting | bytes 1048576
  28.9 0.8 %copy.14 = f32[16,8192]{1,0:T(8,128)} copy(f32[16,8192]{1,0:T(8,128)S(1)} %get-tuple-element.3) | data formatting | bytes 1048576
